TPU v7x, 256 devices: a whole 4x4x8 slice. The times are simulated.
256 devices in a mesh: space: 32 (over x, z), col: 8 (over y, core).
Axes of the slice: x: 4, y: 4, z: 8, core: 2. Of those that a mesh axis runs over, the one named last changes fastest.
Arguments:
- blocks: bfloat16 [2560, 24, 128, 128], P('space', 'col'), may hold values from -0.109375 to 0.109375
- basis_tiles: bfloat16 [2560, 128, 128], P('space'), may hold values from -6 to 6
- weights: float32 [2560, 128], P('space'), may hold values from 0.1 to 1
- neighbour_device: int32 [2560, 24], P('space', 'col'), may hold values from 0 to 31, as said below
- neighbour_row: int32 [2560, 24], P('space', 'col'), may hold values from 0 to 79
- counts: int32 [2560], P('space'), may hold values from 12 to 24
- aggregate: int32 [2560], P('space'), may hold values from 0 to 9
- pair_slot: int32 [2560, 24], P('space', 'col'), may hold values from 0 to 3
Outputs:
- coarse: float32 [1280, 128, 128], P(('space', 'col'))
Inputs may be any that keep to these rules, and one draw needn't show every extreme that they name: `neighbour_device`: among the slots of one device's 80 rows that fall to one index of col, exactly 60 name another device; no other device is named more than 3 times there, and some other device exactly 3 times.
All inputs are finite; a program needn't handle non-finite values.
Results may differ from a plain program's by a relative error of at most 0.0045.
Values may be sent and summed in bfloat16 or wider, within the bound.
A program may use at most 128 MiB of HBM per device.

v0:
```python
import jax
import jax.numpy as jnp
from jax import lax
from jax.sharding import PartitionSpec as P

KC = 4
CAP = 3
NCD = 10


def per_device(
    blocks, basis_tiles, weights, neighbour_device, neighbour_row, counts, aggregate, pair_slot
):
    space_count = lax.axis_size("space")
    own_index = lax.axis_index("space")
    col_index = lax.axis_index("col")
    row_count, slot_count = neighbour_device.shape
    block_size = blocks.shape[2]
    coarse_size = basis_tiles.shape[2]
    slot_total = row_count * slot_count
    peer_of = neighbour_device.reshape(slot_total)
    row_of = neighbour_row.reshape(slot_total)
    remote = peer_of != own_index
    onehot = (
        (peer_of[:, None] == jnp.arange(space_count, dtype=jnp.int32)[None, :]) & remote[:, None]
    ).astype(jnp.int32)
    position = jnp.sum((jnp.cumsum(onehot, axis=0) - onehot) * onehot, axis=1)
    bucket = jnp.where(remote, peer_of * CAP + position, space_count * CAP)
    requests = jnp.zeros((space_count * CAP,), jnp.int32).at[bucket].set(row_of, mode="drop")
    requests = requests.reshape(space_count, CAP)
    asked_rows = lax.all_to_all(requests, "space", split_axis=0, concat_axis=0, tiled=True)
    tile_index = jnp.where(remote, row_count + bucket, row_of)
    received = lax.all_to_all(
        basis_tiles[asked_rows], "space", split_axis=0, concat_axis=0, tiled=True
    )
    tile_table = jnp.concatenate(
        [basis_tiles, received.reshape(space_count * CAP, block_size, coarse_size)], axis=0
    )
    fetched = tile_table[tile_index].reshape(row_count, slot_count, block_size, coarse_size)
    slot_number = col_index * slot_count + jnp.arange(slot_count, dtype=jnp.int32)
    usable = slot_number[None, :] < counts[:, None]
    masked = jnp.where(usable[:, :, None, None], blocks, jnp.zeros((), blocks.dtype))
    partial_sum = jnp.einsum("rkab,rkbc->rac", masked, fetched, preferred_element_type=jnp.float32)
    smoothed = lax.psum(partial_sum, "col")
    prolong = (basis_tiles.astype(jnp.float32) - weights[:, :, None] * smoothed).astype(
        jnp.bfloat16
    )
    received_prolong = lax.all_to_all(
        prolong[asked_rows], "space", split_axis=0, concat_axis=0, tiled=True
    )
    prolong_table = jnp.concatenate(
        [prolong, received_prolong.reshape(space_count * CAP, block_size, coarse_size)], axis=0
    )
    neighbour_prolong = prolong_table[tile_index].reshape(
        row_count, slot_count, block_size, coarse_size
    )
    applied = jnp.einsum(
        "rkab,rkbc->rkac", masked, neighbour_prolong, preferred_element_type=jnp.float32
    ).astype(jnp.bfloat16)
    contribution = jnp.einsum(
        "rad,rkae->rkde", prolong, applied, preferred_element_type=jnp.float32
    )
    targets = (aggregate[:, None] * KC + pair_slot).reshape(slot_total)
    coarse_local = jax.ops.segment_sum(
        contribution.reshape(slot_total, coarse_size, coarse_size), targets, num_segments=NCD * KC
    )
    return lax.psum_scatter(coarse_local, "col", scatter_dimension=0, tiled=True)


def solution(mesh):
    return jax.shard_map(
        per_device,
        mesh=mesh,
        in_specs=(
            P("space", "col", None, None),
            P("space", None, None),
            P("space", None),
            P("space", "col"),
            P("space", "col"),
            P("space"),
            P("space"),
            P("space", "col"),
        ),
        out_specs=P(("space", "col"), None, None),
        check_vma=False,
    )
```

profile of v0, /device:TPU:6, one launch (start us, length us, event | category | flops | bytes accessed | tf_op | source)
XLA Modules:
  0.0 429.7 jit_solution(17318623963266410459)
XLA Ops:
  6.5 0.8 copy.26
  7.3 0.7 broadcast_multiply_fusion
  8.0 0.8 copy.29
  8.9 0.2 reshape.224
  9.1 0.2 eq.22
  9.2 0.7 broadcast_compare_fusion.1
  10.0 0.6 reduce-window.6
  10.6 0.2 slice_reduce_fusion
  11.0 0.2 ne.29
  11.3 0.2 mul.47
  11.5 1.3 scatter_custom_fusion
  12.9 19.3 %all_to_all.22 = s32[32,1,3]{2,1,0:T(1,128)S(1)} all-to-all(s32[32,1,3]{2,1,0:T(1,128)S(1)} %bitcast.44), channel_id=1, replica_groups=mesh['space'=32,'col'=8] {'space'}, dimensions={0} | all-to-all | bytes 768 | tf_op jit(solution)/shard_map/all_to_all | solution.py:31
  32.6 4.6 %gather_fusion = bf16[96,128,128]{2,1,0:T(8,128)(2,1)} fusion(bf16[80,128,128]{2,1,0:T(8,128)(2,1)} %param.9, s32[1024]{0:T(1024)S(1)} %pad_clamp_fusion.1), kind=kCustom, calls=%fused_computation | custom fusion | bytes 6291840 | tf_op jit(solution)/shard_map/gather | solution.py:34
  37.2 6.6 %all-to-all-start.1 = ((bf16[32,3,128,128]{3,2,1,0:T(8,128)(2,1)}), bf16[32,3,128,128]{3,2,1,0:T(8,128)(2,1)}, u32[]{:S(2)}, u32[]{:S(2)}) async-start(bf16[32,3,128,128]{3,2,1,0:T(8,128)(2,1)} %bitcast.41), calls=%async_computation.1 | async-start | bytes 6291456 | tf_op jit(solution)/shard_map/all_to_all | solution.py:33
  44.0 71.3 %all-to-all-done.1 = bf16[32,3,128,128]{3,2,1,0:T(8,128)(2,1)} async-done(((bf16[32,3,128,128]{3,2,1,0:T(8,128)(2,1)}), bf16[32,3,128,128]{3,2,1,0:T(8,128)(2,1)}, u32[]{:S(2)}, u32[]{:S(2)}) %all-to-all-start.1) | async-done | bytes 3145760 | tf_op jit(solution)/shard_map/all_to_all | solution.py:33
  115.3 4.9 %pad_maximum_fusion = bf16[176,128,128]{2,1,0:T(8,128)(2,1)} fusion(bf16[96,128,128]{2,1,0:T(8,128)(2,1)} %bitcast.6, bf16[80,128,128]{2,1,0:T(8,128)(2,1)S(1)} %copy-done.1), kind=kLoop, calls=%fused_computation.11 | loop fusion | flops 2883584 | bytes 11534336 | tf_op jit(solution)/shard_map/concatenate | solution.py:36
  120.2 11.1 %gather_fusion.1 = bf16[240,128,128]{2,1,0:T(8,128)(2,1)} fusion(bf16[176,128,128]{2,1,0:T(8,128)(2,1)} %pad_maximum_fusion, s32[1024]{0:T(1024)S(1)} %pad_clamp_fusion), kind=kCustom, calls=%fused_computation.1 | custom fusion | bytes 15729600 | tf_op jit(solution)/shard_map/gather | solution.py:39
  131.4 10.1 %fusion.8 = f32[80,128,128]{2,1,0:T(8,128)} fusion(bf16[80,3,128,128]{3,2,1,0:T(8,128)(2,1)} %bitcast.43, bf16[80,3,128,128]{3,2,1,0:T(8,128)(2,1)} %param.8, pred[80,3]{1,0:T(8,128)(4,1)S(1)} %broadcast_compare_fusion), kind=kOutput, calls=%fused_computation.17 | convolution fusion | flops 1010565120 | bytes 20971760 | tf_op jit(solution)/shard_map/rkab,rkbc->rac/dot_general | solution.py:43
  141.4 79.2 %all-reduce.3.cloned.1.call-done = f32[80,128,128]{2,1,0:T(8,128)} async-done(((f32[80,128,128]{2,1,0:T(8,128)}), f32[80,128,128]{2,1,0:T(8,128)}) %all-reduce.3.cloned.1.call-update) | async-done | bytes 5242896 | tf_op jit(solution)/shard_map/psum | solution.py:44
  220.7 4.6 %subtract_convert_fusion = bf16[80,128,128]{2,1,0:T(8,128)(2,1)S(1)} fusion(f32[80,128,128]{2,1,0:T(8,128)} %all-reduce.3.cloned.1.call-done, bf16[80,128,128]{2,1,0:T(8,128)(2,1)} %param.9, f32[80,128]{1,0:T(8,128)S(1)} %copy-done.2), kind=kLoop, calls=%fused_computation.13 | loop fusion | flops 5242880 | bytes 10526720 | tf_op jit(solution)/shard_map/convert_element_type | solution.py:45
  225.3 2.7 gather_fusion.2
  228.0 10.2 %all-to-all-start.2 = ((bf16[32,3,128,128]{3,2,1,0:T(8,128)(2,1)}), bf16[32,3,128,128]{3,2,1,0:T(8,128)(2,1)}, u32[]{:S(2)}, u32[]{:S(2)}) async-start(bf16[32,3,128,128]{3,2,1,0:T(8,128)(2,1)} %bitcast.42), calls=%async_computation.2 | async-start | bytes 6291456 | tf_op jit(solution)/shard_map/all_to_all | solution.py:48
  238.3 0.2 reduce-scatter.2.cloned.1.call-start
  238.8 71.7 %all-to-all-done.2 = bf16[32,3,128,128]{3,2,1,0:T(8,128)(2,1)} async-done(((bf16[32,3,128,128]{3,2,1,0:T(8,128)(2,1)}), bf16[32,3,128,128]{3,2,1,0:T(8,128)(2,1)}, u32[]{:S(2)}, u32[]{:S(2)}) %all-to-all-start.2) | async-done | bytes 3145760 | tf_op jit(solution)/shard_map/all_to_all | solution.py:48
  310.5 4.9 %pad_maximum_fusion.1 = bf16[176,128,128]{2,1,0:T(8,128)(2,1)} fusion(bf16[96,128,128]{2,1,0:T(8,128)(2,1)} %bitcast.12, bf16[80,128,128]{2,1,0:T(8,128)(2,1)S(1)} %subtract_convert_fusion), kind=kLoop, calls=%fused_computation.12 | loop fusion | flops 2883584 | bytes 11534336 | tf_op jit(solution)/shard_map/concatenate | solution.py:51
  315.4 11.1 %gather_fusion.3 = bf16[240,128,128]{2,1,0:T(8,128)(2,1)} fusion(bf16[176,128,128]{2,1,0:T(8,128)(2,1)} %pad_maximum_fusion.1, s32[1024]{0:T(1024)S(1)} %pad_clamp_fusion), kind=kCustom, calls=%fused_computation.3 | custom fusion | bytes 15729600 | tf_op jit(solution)/shard_map/gather | solution.py:54
  326.5 11.1 %fusion = f32[80,3,128,128]{3,2,1,0:T(8,128)} fusion(bf16[80,3,128,128]{3,2,1,0:T(8,128)(2,1)} %bitcast.40, bf16[80,3,128,128]{3,2,1,0:T(8,128)(2,1)} %param.8, pred[80,3]{1,0:T(8,128)(4,1)S(1)} %broadcast_compare_fusion, bf16[80,128,128]{2,1,0:T(8,128)(2,1)S(1)} %subtract_convert_fusion), kind=kOutput, calls=%fused_computation.6 | convolution fusion | flops 2021130240 | bytes 34078960 | tf_op jit(solution)/shard_map/rad,rkae->rkde/dot_general | solution.py:60
  337.6 15.7 %copy.35 = f32[240,128,128]{2,1,0:T(8,128)} copy(f32[240,128,128]{1,2,0:T(8,128)} %bitcast.39) | data formatting | bytes 31457280 | tf_op jit(solution)/shard_map/reshape | solution.py:65
  353.3 0.3 broadcast_in_dim.20
  353.6 31.5 %scatter_fusion = f32[40,128,128]{2,1,0:T(8,128)S(1)} fusion(f32[40,128,128]{2,1,0:T(8,128)S(1)} %broadcast_in_dim.20, s32[240]{0:T(256)S(1)} %reshape.230, f32[240,128,128]{2,1,0:T(8,128)} %copy.35), kind=kCustom, calls=%fused_computation.5 | custom fusion | flops 3932160 | bytes 47186880 | tf_op jit(solution)/shard_map/scatter-add | solution.py:64
  385.1 1.5 copy-done
  386.7 36.2 %reduce-scatter.2.cloned.1.call-done = f32[5,128,128]{2,1,0:T(8,128)} async-done(((f32[40,128,128]{2,1,0:T(8,128)}), f32[5,128,128]{2,1,0:T(8,128)}) %reduce-scatter.2.cloned.1.call-update) | async-done | bytes 327696 | tf_op jit(solution)/shard_map/reduce_scatter | solution.py:67
  (38 shorter events, 1.4 us)
Async XLA Ops:
  32.6 11.4 %copy-start.4 = (s32[80]{0:T(128)S(1)}, s32[80]{0:T(128)}, u32[]{:S(2)}) copy-start(s32[80]{0:T(128)} %param.13) | copy-start | bytes 964
  32.6 82.7 %copy-start.1 = (bf16[80,128,128]{2,1,0:T(8,128)(2,1)S(1)}, bf16[80,128,128]{2,1,0:T(8,128)(2,1)}, u32[]{:S(2)}) copy-start(bf16[80,128,128]{2,1,0:T(8,128)(2,1)} %param.9) | copy-start | bytes 7864324
  37.2 78.1 %all-to-all-start.1 = ((bf16[32,3,128,128]{3,2,1,0:T(8,128)(2,1)}), bf16[32,3,128,128]{3,2,1,0:T(8,128)(2,1)}, u32[]{:S(2)}, u32[]{:S(2)}) async-start(bf16[32,3,128,128]{3,2,1,0:T(8,128)(2,1)} %bitcast.41), calls=%async_computation.1 | async-start | bytes 6291456 | tf_op jit(solution)/shard_map/all_to_all | solution.py:33
  43.9 176.8 %all-reduce.3.cloned.1.call-start = ((), (), s32[]{:S(2)}) async-start(), calls=%async_computation.4 | async-start | bytes 10485760 | tf_op jit(solution)/shard_map/psum | solution.py:44
  131.4 89.3 %copy-start.2 = (f32[80,128]{1,0:T(8,128)S(1)}, f32[80,128]{1,0:T(8,128)}, u32[]{:S(2)}) copy-start(f32[80,128]{1,0:T(8,128)} %param.10) | copy-start | bytes 122884
  225.3 13.2 %copy-start.5 = (s32[80]{0:T(128)S(1)}, s32[80]{0:T(128)}, u32[]{:S(2)}) copy-start(s32[80]{0:T(128)} %param.14) | copy-start | bytes 964
  225.3 13.2 %copy-start.3 = (s32[80,3]{0,1:T(4,128)S(1)}, s32[80,3]{0,1:T(4,128)}, u32[]{:S(2)}) copy-start(s32[80,3]{0,1:T(4,128)} %param.15) | copy-start | bytes 2884
  228.0 82.5 %all-to-all-start.2 = ((bf16[32,3,128,128]{3,2,1,0:T(8,128)(2,1)}), bf16[32,3,128,128]{3,2,1,0:T(8,128)(2,1)}, u32[]{:S(2)}, u32[]{:S(2)}) async-start(bf16[32,3,128,128]{3,2,1,0:T(8,128)(2,1)} %bitcast.42), calls=%async_computation.2 | async-start | bytes 6291456 | tf_op jit(solution)/shard_map/all_to_all | solution.py:48
  238.3 184.5 %reduce-scatter.2.cloned.1.call-start = ((), (), s32[]{:S(2)}) async-start(), calls=%async_computation.5 | async-start | bytes 2949120 | tf_op jit(solution)/shard_map/reduce_scatter | solution.py:67
  385.1 1.5 copy-start
Sparse Core Ops, SparseCore 0:
  141.6 79.0 all-reduce.2
  386.8 35.9 reduce-scatter.1
where the time goes:
time: 431 us; the launch traced here: 430 us
  waiting for transfers between devices  258 us (60%)
  local copies, waits for them, and re-layouts  51.8 us (12%)
  other arithmetic  48.2 us (11%)
  matrix products  21.2 us (5%)
  blocking collectives  19.3 us (4%)
  starting transfers between devices  17.1 us (4%)
  between operations  13.6 us (3%)
    psum x1, waiting for transfers between devices, per_device(): smoothed = lax.psum(partial_sum, 'col')  79.2 us
    all_to_all x1, waiting for transfers between devices, per_device(): lax.all_to_all(prolong[asked_rows], 'space', split_axis=0, concat_axis=0,...  71.7 us
    all_to_all x1, waiting for transfers between devices, per_device(): lax.all_to_all(basis_tiles[asked_rows], 'space', split_axis=0, concat_axi...  71.3 us
    reduce_scatter x1, waiting for transfers between devices, per_device(): lax.psum_scatter(coarse_local, 'col', scatter_dimension=0, tiled=True)  36.2 us
    scatter-add x1, other arithmetic, per_device(): jax.ops.segment_sum(contribution.reshape(slot_total, coarse_size, coarse_...  31.5 us
    all_to_all x1, blocking collectives, per_device(): lax.all_to_all(requests, 'space', split_axis=0, concat_axis=0, tiled=True)  19.3 us
    reshape x1, local copies, waits for them, and re-layouts, per_device(): contribution.reshape(slot_total, coarse_size, coarse_size)  15.7 us
    gather x1, local copies, waits for them, and re-layouts, per_device(): prolong_table[tile_index]  11.1 us
  transfers between devices with their start and end apart: 4, of which 4 were waited for; matrix products, arithmetic and copies ran while one was open for 0% of the time, Pallas kernels for 0%

commit v1 on v0

--- a/solution.py
+++ b/solution.py
@@ -41,7 +41,7 @@
     usable = slot_number[None, :] < counts[:, None]
     masked = jnp.where(usable[:, :, None, None], blocks, jnp.zeros((), blocks.dtype))
     partial_sum = jnp.einsum("rkab,rkbc->rac", masked, fetched, preferred_element_type=jnp.float32)
-    smoothed = lax.psum(partial_sum, "col")
+    smoothed = jnp.sum(lax.all_gather(partial_sum, "col"), axis=0)
     prolong = (basis_tiles.astype(jnp.float32) - weights[:, :, None] * smoothed).astype(
         jnp.bfloat16
     )

time: 431 us -> 560 us (1.30)
  waiting for transfers between devices: 258 us -> 370 us
  other arithmetic: 48.2 us -> 65.4 us
    all_gather x0 -> x1, waiting for transfers between devices: none -> 193 us  [per_device(): smoothed = jnp.sum(lax.all_gather(partial_sum, 'col'), axis=0)]
    psum x1 -> x0, waiting for transfers between devices: 79.2 us -> none  [per_device(): smoothed = lax.psum(partial_sum, 'col')]
    reduce_sum x0 -> x1, other arithmetic: none -> 17.3 us  [per_device(): smoothed = jnp.sum(lax.all_gather(partial_sum, 'col'), axis=0)]
where the time goes in v1:
time: 560 us; the launch traced here: 559 us
  waiting for transfers between devices  370 us (66%)
  other arithmetic  65.4 us (12%)
  local copies, waits for them, and re-layouts  51.8 us (9%)
  matrix products  21.2 us (4%)
  blocking collectives  19.3 us (3%)
  starting transfers between devices  17.1 us (3%)
  between operations  13.6 us (2%)
    all_gather x1, waiting for transfers between devices, per_device(): smoothed = jnp.sum(lax.all_gather(partial_sum, 'col'), axis=0)  193 us
    all_to_all x1, waiting for transfers between devices, per_device(): lax.all_to_all(basis_tiles[asked_rows], 'space', split_axis=0, concat_axi...  71.3 us
    all_to_all x1, waiting for transfers between devices, per_device(): lax.all_to_all(prolong[asked_rows], 'space', split_axis=0, concat_axis=0,...  71.2 us
    reduce_scatter x1, waiting for transfers between devices, per_device(): lax.psum_scatter(coarse_local, 'col', scatter_dimension=0, tiled=True)  35 us
    scatter-add x1, other arithmetic, per_device(): jax.ops.segment_sum(contribution.reshape(slot_total, coarse_size, coarse_...  31.5 us
    all_to_all x1, blocking collectives, per_device(): lax.all_to_all(requests, 'space', split_axis=0, concat_axis=0, tiled=True)  19.3 us
    reduce_sum x1, other arithmetic, per_device(): smoothed = jnp.sum(lax.all_gather(partial_sum, 'col'), axis=0)  17.3 us
    reshape x1, local copies, waits for them, and re-layouts, per_device(): contribution.reshape(slot_total, coarse_size, coarse_size)  15.7 us
  transfers between devices with their start and end apart: 4, of which 4 were waited for; matrix products, arithmetic and copies ran while one was open for 0% of the time, Pallas kernels for 0%

profile of v1, /device:TPU:6, one launch (start us, length us, event | category | flops | bytes accessed | tf_op | source)
XLA Modules:
  0.0 558.7 jit_solution(11857731498358065532)
XLA Ops:
  6.5 0.8 copy.26
  7.3 0.7 broadcast_multiply_fusion
  8.0 0.8 copy.29
  9.1 0.2 eq.22
  9.2 0.7 broadcast_compare_fusion.1
  10.0 0.6 reduce-window.6
  10.6 0.2 slice_reduce_fusion
  11.0 0.2 ne.29
  11.3 0.2 mul.47
  11.5 1.3 scatter_custom_fusion
  12.9 19.3 %all_to_all.22 = s32[32,1,3]{2,1,0:T(1,128)S(1)} all-to-all(s32[32,1,3]{2,1,0:T(1,128)S(1)} %bitcast.46), channel_id=1, replica_groups=mesh['space'=32,'col'=8] {'space'}, dimensions={0} | all-to-all | bytes 768 | tf_op jit(solution)/shard_map/all_to_all | solution.py:31
  32.6 4.6 gather_fusion
  37.2 6.6 %all-to-all-start.1 = ((bf16[32,3,128,128]{3,2,1,0:T(8,128)(2,1)}), bf16[32,3,128,128]{3,2,1,0:T(8,128)(2,1)}, u32[]{:S(2)}, u32[]{:S(2)}) async-start(bf16[32,3,128,128]{3,2,1,0:T(8,128)(2,1)} %bitcast.43), calls=%async_computation.1 | async-start | bytes 6291456 | tf_op jit(solution)/shard_map/all_to_all | solution.py:33
  44.0 71.3 %all-to-all-done.1 = bf16[32,3,128,128]{3,2,1,0:T(8,128)(2,1)} async-done(((bf16[32,3,128,128]{3,2,1,0:T(8,128)(2,1)}), bf16[32,3,128,128]{3,2,1,0:T(8,128)(2,1)}, u32[]{:S(2)}, u32[]{:S(2)}) %all-to-all-start.1) | async-done | bytes 3145760 | tf_op jit(solution)/shard_map/all_to_all | solution.py:33
  115.3 4.9 pad_maximum_fusion
  120.2 11.1 %gather_fusion.1 = bf16[240,128,128]{2,1,0:T(8,128)(2,1)} fusion(bf16[176,128,128]{2,1,0:T(8,128)(2,1)} %pad_maximum_fusion, s32[1024]{0:T(1024)S(1)} %pad_clamp_fusion), kind=kCustom, calls=%fused_computation.1 | custom fusion | bytes 15729600 | tf_op jit(solution)/shard_map/gather | solution.py:39
  131.4 10.1 %fusion.8 = f32[80,128,128]{2,1,0:T(8,128)} fusion(bf16[80,3,128,128]{3,2,1,0:T(8,128)(2,1)} %bitcast.45, bf16[80,3,128,128]{3,2,1,0:T(8,128)(2,1)} %param.8, pred[80,3]{1,0:T(8,128)(4,1)S(1)} %broadcast_compare_fusion), kind=kOutput, calls=%fused_computation.17 | convolution fusion | flops 1010565120 | bytes 20971760 | tf_op jit(solution)/shard_map/rkab,rkbc->rac/dot_general | solution.py:43
  141.5 192.7 %all-gather.3.cloned.1.call-done = f32[640,128,128]{2,1,0:T(8,128)} async-done(((f32[80,128,128]{2,1,0:T(8,128)}), f32[640,128,128]{2,1,0:T(8,128)}) %all-gather.3.cloned.1.call-update) | async-done | bytes 41943056 | tf_op jit(solution)/shard_map/all_gather | solution.py:44
  334.2 17.3 %reduce_sum.22 = f32[80,128,128]{2,1,0:T(8,128)} reduce(f32[8,80,128,128]{3,2,1,0:T(8,128)} %bitcast.41, f32[]{:T(128)} %constant.12.clone.1), dimensions={0}, to_apply=%region_4.5 | reduce | flops 9175040 | bytes 47185924 | tf_op jit(solution)/shard_map/reduce_sum | solution.py:44
  351.4 4.6 subtract_convert_fusion
  356.1 2.7 gather_fusion.2
  358.8 10.2 %all-to-all-start.2 = ((bf16[32,3,128,128]{3,2,1,0:T(8,128)(2,1)}), bf16[32,3,128,128]{3,2,1,0:T(8,128)(2,1)}, u32[]{:S(2)}, u32[]{:S(2)}) async-start(bf16[32,3,128,128]{3,2,1,0:T(8,128)(2,1)} %bitcast.44), calls=%async_computation.2 | async-start | bytes 6291456 | tf_op jit(solution)/shard_map/all_to_all | solution.py:48
  369.0 0.2 reduce-scatter.2.cloned.1.call-start
  369.5 71.2 %all-to-all-done.2 = bf16[32,3,128,128]{3,2,1,0:T(8,128)(2,1)} async-done(((bf16[32,3,128,128]{3,2,1,0:T(8,128)(2,1)}), bf16[32,3,128,128]{3,2,1,0:T(8,128)(2,1)}, u32[]{:S(2)}, u32[]{:S(2)}) %all-to-all-start.2) | async-done | bytes 3145760 | tf_op jit(solution)/shard_map/all_to_all | solution.py:48
  440.7 4.9 pad_maximum_fusion.1
  445.6 11.1 %gather_fusion.3 = bf16[240,128,128]{2,1,0:T(8,128)(2,1)} fusion(bf16[176,128,128]{2,1,0:T(8,128)(2,1)} %pad_maximum_fusion.1, s32[1024]{0:T(1024)S(1)} %pad_clamp_fusion), kind=kCustom, calls=%fused_computation.3 | custom fusion | bytes 15729600 | tf_op jit(solution)/shard_map/gather | solution.py:54
  456.7 11.1 %fusion = f32[80,3,128,128]{3,2,1,0:T(8,128)} fusion(bf16[80,3,128,128]{3,2,1,0:T(8,128)(2,1)} %bitcast.42, bf16[80,3,128,128]{3,2,1,0:T(8,128)(2,1)} %param.8, pred[80,3]{1,0:T(8,128)(4,1)S(1)} %broadcast_compare_fusion, bf16[80,128,128]{2,1,0:T(8,128)(2,1)S(1)} %subtract_convert_fusion), kind=kOutput, calls=%fused_computation.6 | convolution fusion | flops 2021130240 | bytes 34078960 | tf_op jit(solution)/shard_map/rad,rkae->rkde/dot_general | solution.py:60
  467.8 15.7 %copy.35 = f32[240,128,128]{2,1,0:T(8,128)} copy(f32[240,128,128]{1,2,0:T(8,128)} %bitcast.40) | data formatting | bytes 31457280 | tf_op jit(solution)/shard_map/reshape | solution.py:65
  483.5 0.3 broadcast_in_dim.20
  483.8 31.5 %scatter_fusion = f32[40,128,128]{2,1,0:T(8,128)S(1)} fusion(f32[40,128,128]{2,1,0:T(8,128)S(1)} %broadcast_in_dim.20, s32[240]{0:T(256)S(1)} %reshape.230, f32[240,128,128]{2,1,0:T(8,128)} %copy.35), kind=kCustom, calls=%fused_computation.5 | custom fusion | flops 3932160 | bytes 47186880 | tf_op jit(solution)/shard_map/scatter-add | solution.py:64
  515.3 1.5 copy-done
  516.9 35.0 %reduce-scatter.2.cloned.1.call-done = f32[5,128,128]{2,1,0:T(8,128)} async-done(((f32[40,128,128]{2,1,0:T(8,128)}), f32[5,128,128]{2,1,0:T(8,128)}) %reduce-scatter.2.cloned.1.call-update) | async-done | bytes 327696 | tf_op jit(solution)/shard_map/reduce_scatter | solution.py:67
  (39 shorter events, 1.6 us)
Async XLA Ops:
  32.6 11.4 %copy-start.4 = (s32[80]{0:T(128)S(1)}, s32[80]{0:T(128)}, u32[]{:S(2)}) copy-start(s32[80]{0:T(128)} %param.13) | copy-start | bytes 964
  32.6 82.7 %copy-start.1 = (bf16[80,128,128]{2,1,0:T(8,128)(2,1)S(1)}, bf16[80,128,128]{2,1,0:T(8,128)(2,1)}, u32[]{:S(2)}) copy-start(bf16[80,128,128]{2,1,0:T(8,128)(2,1)} %param.9) | copy-start | bytes 7864324
  37.2 78.1 %all-to-all-start.1 = ((bf16[32,3,128,128]{3,2,1,0:T(8,128)(2,1)}), bf16[32,3,128,128]{3,2,1,0:T(8,128)(2,1)}, u32[]{:S(2)}, u32[]{:S(2)}) async-start(bf16[32,3,128,128]{3,2,1,0:T(8,128)(2,1)} %bitcast.43), calls=%async_computation.1 | async-start | bytes 6291456 | tf_op jit(solution)/shard_map/all_to_all | solution.py:33
  43.9 290.3 %all-gather.3.cloned.1.call-start = ((), (), s32[]{:S(2)}) async-start(), calls=%async_computation.5 | async-start | bytes 47185920 | tf_op jit(solution)/shard_map/all_gather | solution.py:44
  334.2 17.3 %copy-start.2 = (f32[80,128]{1,0:T(8,128)S(1)}, f32[80,128]{1,0:T(8,128)}, u32[]{:S(2)}) copy-start(f32[80,128]{1,0:T(8,128)} %param.10) | copy-start | bytes 122884
  356.0 13.2 %copy-start.5 = (s32[80]{0:T(128)S(1)}, s32[80]{0:T(128)}, u32[]{:S(2)}) copy-start(s32[80]{0:T(128)} %param.14) | copy-start | bytes 964
  356.1 13.2 %copy-start.3 = (s32[80,3]{0,1:T(4,128)S(1)}, s32[80,3]{0,1:T(4,128)}, u32[]{:S(2)}) copy-start(s32[80,3]{0,1:T(4,128)} %param.15) | copy-start | bytes 2884
  358.8 82.0 %all-to-all-start.2 = ((bf16[32,3,128,128]{3,2,1,0:T(8,128)(2,1)}), bf16[32,3,128,128]{3,2,1,0:T(8,128)(2,1)}, u32[]{:S(2)}, u32[]{:S(2)}) async-start(bf16[32,3,128,128]{3,2,1,0:T(8,128)(2,1)} %bitcast.44), calls=%async_computation.2 | async-start | bytes 6291456 | tf_op jit(solution)/shard_map/all_to_all | solution.py:48
  369.0 182.9 %reduce-scatter.2.cloned.1.call-start = ((), (), s32[]{:S(2)}) async-start(), calls=%async_computation.4 | async-start | bytes 2949120 | tf_op jit(solution)/shard_map/reduce_scatter | solution.py:67
  515.3 1.5 copy-start
Sparse Core Ops, SparseCore 0:
  141.6 192.5 all-gather.2
  517.0 34.8 reduce-scatter.1
